TPU v7x, 256 devices: a whole 4x4x8 slice. The times are simulated.
256 devices in a mesh: samples: 64 (over z, y, x_lo), vblocks: 4 (over x_hi, core).
Axes of the slice: x: 4 (x_hi: 2, x_lo: 2; x = x_hi * 2 + x_lo), y: 4, z: 8, core: 2. Of those that a mesh axis runs over, the one named last changes fastest.
Arguments:
- genotypes: int32 [65536, 4096], P('samples', 'vblocks'), may hold values from 0 to 2
- typed_mask: int32 [4096], P('vblocks'), may hold values 0 or 1
- z_scores: float32 [1024, 4096], P('samples', 'vblocks'), may hold values from -60 to 60
Outputs:
- solution: float32 [1024, 4096], P('samples', 'vblocks')
- imputed: float32 [1024, 4096], P('samples', 'vblocks')
All inputs are finite; a program needn't handle non-finite values. No bound on the sum of `typed_mask` on one device may be relied on, other than what follows from the above.
Results may differ from a plain program's by a relative error of at most 0.0068.
Values may be sent and summed in bfloat16 or wider, within the bound.
No kernel may reach another device: no remote copies, remote signals or barrier semaphores. Data moves between devices by JAX's collectives and lax.ppermute only.
A program may use at most 64 MiB of HBM per device.

v0:
```python
import jax
import jax.numpy as jnp
from jax import lax
from jax.sharding import PartitionSpec as P

ITERS = 3


RIDGE = 0.1
EPSILON = 1e-05
HIGHEST = lax.Precision.HIGHEST


def passed_along(block, axis, distance):
    devices = range(lax.axis_size(axis))
    route = [(i - distance, i) for i in devices if i - distance in devices]
    return lax.ppermute(block, axis, route)


def contract_rows(first_mat, second_mat):
    return lax.dot_general(
        first_mat, second_mat, (((0,), (0,)), ((), ())), preferred_element_type=jnp.float32
    )


def times_transpose(vector, matrix):
    return lax.dot_general(
        vector,
        matrix,
        (((1,), (1,)), ((), ())),
        precision=HIGHEST,
        preferred_element_type=jnp.float32,
    )


def local_sums(first_vec, second_vec):
    return jnp.sum(first_vec * second_vec, axis=1)


def on_device(genotypes, typed_mask, z_scores):
    samples_dev, block_width = genotypes.shape
    total_samples = samples_dev * lax.axis_size("samples")
    dosage = genotypes.astype(jnp.float32)
    totals, squares = lax.psum(
        (jnp.sum(dosage, axis=0), jnp.sum(dosage * dosage, axis=0)), "samples"
    )
    mean_dosage = totals / total_samples
    variance = squares / total_samples - mean_dosage * mean_dosage
    standard = ((dosage - mean_dosage) * lax.rsqrt(variance + EPSILON)).astype(jnp.bfloat16)
    following = passed_along(standard, "vblocks", -1)
    joined = jnp.concatenate([standard, following], axis=1)
    summed = lax.psum_scatter(
        contract_rows(standard, joined), "samples", scatter_dimension=0, tiled=True
    )
    link_rows = (summed / total_samples).astype(jnp.bfloat16)
    gathered = lax.all_gather(link_rows, "samples", axis=0, tiled=True)
    own_block = gathered[:, :block_width].astype(jnp.float32)
    edge_half = gathered[:, block_width:]
    edge_block = edge_half.astype(jnp.float32)

    def apply_link(vector):
        ahead_part = passed_along(vector, "vblocks", -1)
        outgoing = jnp.dot(
            vector, edge_block, precision=HIGHEST, preferred_element_type=jnp.float32
        )
        lower_part = passed_along(outgoing, "vblocks", 1)
        result = times_transpose(vector, own_block)
        result = result + 0.5 * times_transpose(ahead_part, edge_block)
        return result + 0.5 * lower_part

    mask_row = typed_mask.astype(jnp.float32)[None, :]
    right_side = mask_row * z_scores
    solution = jnp.zeros_like(right_side)
    residual = right_side

    def squares_sum(vector):
        return lax.psum(local_sums(vector, vector), "vblocks")

    direction = right_side
    norm_now = squares_sum(residual)
    for iteration in range(ITERS):
        image = mask_row * apply_link(mask_row * direction) + RIDGE * direction
        step_size = norm_now / lax.psum(local_sums(direction, image), "vblocks")
        solution = solution + step_size[:, None] * direction
        residual = residual - step_size[:, None] * image
        if iteration + 1 < ITERS:
            norm_next = squares_sum(residual)
            direction = residual + (norm_next / norm_now)[:, None] * direction
            norm_now = norm_next
    projected = apply_link(mask_row * solution)
    imputed = jnp.where(typed_mask[None, :] == 1, z_scores, projected)
    return (solution, imputed)


def solution(mesh):
    placed = (P("samples", "vblocks"), P("vblocks"), P("samples", "vblocks"))
    return jax.shard_map(
        on_device,
        mesh=mesh,
        in_specs=placed,
        out_specs=(P("samples", "vblocks"), P("samples", "vblocks")),
        check_vma=False,
    )
```

profile of v0, /device:TPU:1, one launch (start us, length us, event | category | flops | bytes accessed | tf_op | source)
XLA Modules:
  0.0 945.3 jit_solution(10318953864122489320)
XLA Ops:
  10.0 136.7 %all-reduce = (f32[1024]{0:T(1024)S(1)}, f32[1024]{0:T(1024)S(1)}) all-reduce(f32[1024]{0:T(1024)S(1)} %get-tuple-element.3, f32[1024]{0:T(1024)S(1)} %get-tuple-element.2), channel_id=1, replica_groups=mesh['samples'=64,'vblocks'=4] {'samples'}, use_global_device_ids=true, to_apply=%region_5.0 | all-reduce | flops 2048 | bytes 16384 | tf_op jit(solution)/shard_map/psum | solution.py:44
  146.7 2.8 multiply_convert_fusion
  149.5 30.3 %collective-permute-start = (bf16[1024,1024]{1,0:T(8,128)(2,1)S(1)}, bf16[1024,1024]{1,0:T(8,128)(2,1)S(1)}, u32[]{:S(2)}, u32[]{:S(2)}) collective-permute-start(bf16[1024,1024]{1,0:T(8,128)(2,1)S(1)} %multiply_convert_fusion), channel_id=1, source_target_pairs={{1,0},{2,1},{3,2},{5,4},{6,5},{7,6},{9,8},{10,9},{11,10},{13,12},{... | collective-permute-start | bytes 6291464 | tf_op jit(solution)/shard_map/ppermute | solution.py:17
  179.9 26.1 %collective-permute-done = bf16[1024,1024]{1,0:T(8,128)(2,1)S(1)} collective-permute-done((bf16[1024,1024]{1,0:T(8,128)(2,1)S(1)}, bf16[1024,1024]{1,0:T(8,128)(2,1)S(1)}, u32[]{:S(2)}, u32[]{:S(2)}) %collective-permute-start) | collective-permute-done | bytes 2097184 | tf_op jit(solution)/shard_map/ppermute | solution.py:17
  206.0 7.0 fusion
  213.1 280.4 %reduce-scatter.2.cloned.1.call-done = f32[16,2048]{1,0:T(8,128)} async-done(((f32[1024,2048]{1,0:T(8,128)}), f32[16,2048]{1,0:T(8,128)}) %reduce-scatter.2.cloned.1.call-update) | async-done | bytes 131088 | tf_op jit(solution)/shard_map/reduce_scatter | solution.py:52
  495.2 50.4 %collective-permute-start.1 = (f32[16,1024]{1,0:T(8,128)S(1)}, f32[16,1024]{1,0:T(8,128)S(1)}, u32[]{:S(2)}, u32[]{:S(2)}) collective-permute-start(f32[16,1024]{1,0:T(8,128)S(1)} %multiply_multiply_fusion), channel_id=1, source_target_pairs={{1,0},{2,1},{3,2},{5,4},{6,5},{7,6},{9,8},{10,9},{11,10},{13,12},{... | collective-permute-start | bytes 196616 | tf_op jit(solution)/shard_map/ppermute | solution.py:17
  545.5 251.5 %all-gather.2.cloned.1.call-done = bf16[1024,2048]{1,0:T(8,128)(2,1)} async-done(((bf16[16,2048]{1,0:T(8,128)(2,1)}), bf16[1024,2048]{1,0:T(8,128)(2,1)}) %all-gather.2.cloned.1.call-update) | async-done | bytes 4194320 | tf_op jit(solution)/shard_map/all_gather | solution.py:56
  799.7 50.3 %collective-permute-start.2 = (f32[16,1024]{1,0:T(8,128)S(1)}, f32[16,1024]{1,0:T(8,128)S(1)}, u32[]{:S(2)}, u32[]{:S(2)}) collective-permute-start(f32[16,1024]{1,0:T(8,128)S(1)} %fusion.38), channel_id=1, source_target_pairs={{0,1},{1,2},{2,3},{4,5},{5,6},{6,7},{8,9},{9,10},{10,11},{12,13},{... | collective-permute-start | bytes 196616 | tf_op jit(solution)/shard_map/ppermute | solution.py:17
  850.1 3.3 fusion.10
  855.3 6.6 all-reduce.1
  862.1 7.6 psum.60
  869.8 4.0 collective-permute-start.3
  876.3 3.6 collective-permute-start.4
  879.9 3.3 fusion.8
  885.1 6.6 psum.61
  891.9 7.6 psum.62
  899.6 4.2 collective-permute-start.5
  906.3 3.6 collective-permute-start.6
  909.9 3.3 fusion.6
  915.1 6.6 psum.63
  922.4 3.1 collective-permute-start.7
  928.0 4.7 collective-permute-start.8
  932.7 3.3 fusion.4
  (48 shorter events, 24.0 us)
Async XLA Ops:
  7.2 486.4 %reduce-scatter.2.cloned.1.call-start = ((), (), s32[]{:S(2)}) async-start(), calls=%async_computation.1 | async-start | bytes 8519680 | tf_op jit(solution)/shard_map/reduce_scatter | solution.py:52
  149.5 56.5 %collective-permute-start = (bf16[1024,1024]{1,0:T(8,128)(2,1)S(1)}, bf16[1024,1024]{1,0:T(8,128)(2,1)S(1)}, u32[]{:S(2)}, u32[]{:S(2)}) collective-permute-start(bf16[1024,1024]{1,0:T(8,128)(2,1)S(1)} %multiply_convert_fusion), channel_id=1, source_target_pairs={{1,0},{2,1},{3,2},{5,4},{6,5},{7,6},{9,8},{10,9},{11,10},{13,12},{... | collective-permute-start | bytes 6291464 | tf_op jit(solution)/shard_map/ppermute | solution.py:17
  213.0 282.1 %copy-start.5 = (s32[1024]{0:T(1024)S(1)}, s32[1024]{0:T(1024)}, u32[]{:S(2)}) copy-start(s32[1024]{0:T(1024)} %param.4) | copy-start | bytes 12292
  213.0 282.1 %copy-start.4 = (f32[16,1024]{1,0:T(8,128)S(1)}, f32[16,1024]{1,0:T(8,128)}, u32[]{:S(2)}) copy-start(f32[16,1024]{1,0:T(8,128)} %param.5) | copy-start | bytes 196612
  213.0 584.0 %all-gather.2.cloned.1.call-start = ((), (), s32[]{:S(2)}) async-start(), calls=%async_computation.2 | async-start | bytes 4259840 | tf_op jit(solution)/shard_map/all_gather | solution.py:56
  495.2 358.2 %collective-permute-start.1 = (f32[16,1024]{1,0:T(8,128)S(1)}, f32[16,1024]{1,0:T(8,128)S(1)}, u32[]{:S(2)}, u32[]{:S(2)}) collective-permute-start(f32[16,1024]{1,0:T(8,128)S(1)} %multiply_multiply_fusion), channel_id=1, source_target_pairs={{1,0},{2,1},{3,2},{5,4},{6,5},{7,6},{9,8},{10,9},{11,10},{13,12},{... | collective-permute-start | bytes 196616 | tf_op jit(solution)/shard_map/ppermute | solution.py:17
  797.0 56.4 %copy-start = (bf16[1024,2048]{1,0:T(8,128)(2,1)S(1)}, bf16[1024,2048]{1,0:T(8,128)(2,1)}, u32[]{:S(2)}) copy-start(bf16[1024,2048]{1,0:T(8,128)(2,1)} %all-gather.2.cloned.1.call-done) | copy-start | bytes 12582916
  799.7 53.7 %collective-permute-start.2 = (f32[16,1024]{1,0:T(8,128)S(1)}, f32[16,1024]{1,0:T(8,128)S(1)}, u32[]{:S(2)}, u32[]{:S(2)}) collective-permute-start(f32[16,1024]{1,0:T(8,128)S(1)} %fusion.38), channel_id=1, source_target_pairs={{0,1},{1,2},{2,3},{4,5},{5,6},{6,7},{8,9},{9,10},{10,11},{12,13},{... | collective-permute-start | bytes 196616 | tf_op jit(solution)/shard_map/ppermute | solution.py:17
  869.7 13.6 %copy-start.1 = (bf16[1024,2048]{1,0:T(8,128)(2,1)S(1)}, bf16[1024,2048]{1,0:T(8,128)(2,1)}, u32[]{:S(2)}) copy-start(bf16[1024,2048]{1,0:T(8,128)(2,1)} %all-gather.2.cloned.1.call-done) | copy-start | bytes 12582916
  869.8 13.4 %collective-permute-start.3 = (f32[16,1024]{1,0:T(8,128)S(1)}, f32[16,1024]{1,0:T(8,128)S(1)}, u32[]{:S(2)}, u32[]{:S(2)}) collective-permute-start(f32[16,1024]{1,0:T(8,128)S(1)} %get-tuple-element.14), channel_id=1, source_target_pairs={{1,0},{2,1},{3,2},{5,4},{6,5},{7,6},{9,8},{10,9},{11,10},{13,12},{... | collective-permute-start | bytes 196616 | tf_op jit(solution)/shard_map/ppermute | solution.py:17
  876.3 6.9 collective-permute-start.4
  899.5 13.7 %copy-start.2 = (bf16[1024,2048]{1,0:T(8,128)(2,1)S(1)}, bf16[1024,2048]{1,0:T(8,128)(2,1)}, u32[]{:S(2)}) copy-start(bf16[1024,2048]{1,0:T(8,128)(2,1)} %all-gather.2.cloned.1.call-done) | copy-start | bytes 12582916
  899.6 13.6 %collective-permute-start.5 = (f32[16,1024]{1,0:T(8,128)S(1)}, f32[16,1024]{1,0:T(8,128)S(1)}, u32[]{:S(2)}, u32[]{:S(2)}) collective-permute-start(f32[16,1024]{1,0:T(8,128)S(1)} %get-tuple-element.12), channel_id=1, source_target_pairs={{1,0},{2,1},{3,2},{5,4},{6,5},{7,6},{9,8},{10,9},{11,10},{13,12},{... | collective-permute-start | bytes 196616 | tf_op jit(solution)/shard_map/ppermute | solution.py:17
  906.3 6.9 collective-permute-start.6
  921.7 14.3 %copy-start.3 = (bf16[1024,2048]{1,0:T(8,128)(2,1)S(1)}, bf16[1024,2048]{1,0:T(8,128)(2,1)}, u32[]{:S(2)}) copy-start(bf16[1024,2048]{1,0:T(8,128)(2,1)} %all-gather.2.cloned.1.call-done) | copy-start | bytes 12582916
  922.4 13.6 %collective-permute-start.7 = (f32[16,1024]{1,0:T(8,128)S(1)}, f32[16,1024]{1,0:T(8,128)S(1)}, u32[]{:S(2)}, u32[]{:S(2)}) collective-permute-start(f32[16,1024]{1,0:T(8,128)S(1)} %get-tuple-element.10), channel_id=1, source_target_pairs={{1,0},{2,1},{3,2},{5,4},{6,5},{7,6},{9,8},{10,9},{11,10},{13,12},{... | collective-permute-start | bytes 196616 | tf_op jit(solution)/shard_map/ppermute | solution.py:17
  928.0 8.0 collective-permute-start.8
Sparse Core Ops, SparseCore 0:
  213.2 280.3 reduce-scatter.1
  495.9 301.1 all-gather.1
where the time goes:
time: 946 us; the launch traced here: 945 us
  waiting for transfers between devices  558 us (59%)
  blocking collectives  172 us (18%)
  starting transfers between devices  154 us (16%)
  matrix products  38.4 us (4%)
  between operations  14.3 us (2%)
    reduce_scatter x1, waiting for transfers between devices, on_device(): lax.psum_scatter(contract_rows(standard, joined), 'samples', scatter_dime...  280 us
    all_gather x1, waiting for transfers between devices, on_device(): gathered = lax.all_gather(link_rows, 'samples', axis=0, tiled=True)  252 us
    ppermute x9, starting transfers between devices, passed_along(): return lax.ppermute(block, axis, route)  154 us
    psum x1, blocking collectives, on_device(): lax.psum((jnp.sum(dosage, axis=0), jnp.sum(dosage * dosage, axis=0)), 'sa...  137 us
    ppermute x9, waiting for transfers between devices, passed_along(): return lax.ppermute(block, axis, route)  26.2 us
    psum x3, blocking collectives, squares_sum(): return lax.psum(local_sums(vector, vector), 'vblocks')  21.8 us
    dot_general x8, matrix products, times_transpose(): lax.dot_general(vector, matrix, (((1,), (1,)), ((), ())), precision=HIGHE...  21.2 us
  transfers between devices with their start and end apart: 11, of which 3 were waited for; matrix products, arithmetic and copies ran while one was open for 2% of the time, Pallas kernels for 0%

commit v1 on v0

v1 whole, which is shorter than its diff:
```python
import jax
import jax.numpy as jnp
from jax import lax
from jax.sharding import Mesh, PartitionSpec as P

ITERS = 3
RIDGE = 0.1
EPSILON = 1e-05
HIGHEST = lax.Precision.HIGHEST
BF16 = jnp.bfloat16
F32 = jnp.float32

SAMPLE_AXES = ("z", "y", "xl")
BLOCK_AXES = ("xh", "core")
N_BLOCKS = 4


def from_next(block):
    return lax.ppermute(block, BLOCK_AXES, [(i + 1, i) for i in range(N_BLOCKS - 1)])


def from_previous(block):
    return lax.ppermute(block, BLOCK_AXES, [(i, i + 1) for i in range(N_BLOCKS - 1)])


def contract_rows(first_mat, second_mat):
    return lax.dot_general(
        first_mat, second_mat, (((0,), (0,)), ((), ())), preferred_element_type=F32
    )


def rounded(values):
    return lax.reduce_precision(values, exponent_bits=8, mantissa_bits=7)


def split3(vector):
    high = rounded(vector)
    rest = vector - high
    mid = rounded(rest)
    return jnp.concatenate([high, mid, rest - mid], axis=0).astype(BF16)


def join3(stacked):
    rows = stacked.shape[0] // 3
    return stacked[2 * rows :] + stacked[rows : 2 * rows] + stacked[:rows]


def times(vector, matrix, side):
    out = lax.dot_general(
        split3(vector), matrix, (((1,), (side,)), ((), ())), preferred_element_type=F32
    )
    return join3(out)


def gather_stats(local_sums, local_squares):
    sums, squares = local_sums, local_squares
    for axis in ("z", "y", "xl"):
        packed = jnp.concatenate([sums, squares], axis=0)[None]
        packed = lax.all_gather(packed, axis, axis=0, tiled=True)
        sums = packed[:, :-1].reshape(-1, packed.shape[-1])
        squares = jnp.sum(packed[:, -1], axis=0, keepdims=True)
    return sums, squares


def line_of(all_sums, all_squares, total_samples):
    coded_sum = jnp.sum(all_sums, axis=0, keepdims=True)
    mean_dosage = (coded_sum + total_samples) / total_samples
    squares = all_squares + 2.0 * coded_sum + total_samples
    variance = squares / total_samples - mean_dosage * mean_dosage
    scale = lax.rsqrt(variance + EPSILON)
    twos = 0.5 * (all_squares + coded_sum)
    zeros = 0.5 * (all_squares - coded_sum)
    ones = total_samples - all_squares
    level = rise = spread = 0.0
    for dosage, count in ((0.0, zeros), (1.0, ones), (2.0, twos)):
        away = dosage - mean_dosage
        value = rounded(away * scale)
        level = level + count * value
        rise = rise + count * value * away
        spread = spread + count * away * away
    slope = jnp.where(spread > 0.0, rise / jnp.where(spread > 0.0, spread, 1.0), scale)
    return level / total_samples, slope


def on_device(genotypes, typed_mask, z_scores):
    samples_dev, width = genotypes.shape
    n_dev = lax.axis_size(SAMPLE_AXES)
    total_samples = samples_dev * n_dev
    coded = (genotypes - 1).astype(BF16)
    following = from_next(coded)
    joined = jnp.concatenate([coded, following], axis=1)
    joined_f = joined.astype(F32)
    sums = jnp.sum(joined_f, axis=0, keepdims=True)
    squares = jnp.sum(joined_f * joined_f, axis=0, keepdims=True)
    counts = contract_rows(coded, joined)
    centred = (counts - sums[0, :width, None] * (sums / samples_dev)).astype(BF16)

    within = lax.psum_scatter(centred, "z", scatter_dimension=0, tiled=True)
    within = lax.psum_scatter(within.astype(F32), "y", scatter_dimension=0, tiled=True)
    within = lax.psum_scatter(within, "xl", scatter_dimension=0, tiled=True)

    all_sums, all_squares = gather_stats(sums, squares)
    level, slope = line_of(all_sums, all_squares, total_samples)
    off = (all_sums - jnp.mean(all_sums, axis=0, keepdims=True)) * slope
    rows = within.shape[0]
    start = lax.axis_index(SAMPLE_AXES) * rows
    off_rows = lax.dynamic_slice_in_dim(off, start, rows, axis=1)
    slope_rows = lax.dynamic_slice_in_dim(slope, start, rows, axis=1)
    level_rows = lax.dynamic_slice_in_dim(level, start, rows, axis=1)
    between = lax.dot_general(
        off_rows, off, (((0,), (0,)), ((), ())), precision=HIGHEST, preferred_element_type=F32
    )
    link = (within * slope * slope_rows[0][:, None] + between / samples_dev) / total_samples
    link = link + level_rows[0][:, None] * level
    link_rows = link.astype(BF16)

    gathered = lax.all_gather(link_rows, "xl", axis=0, tiled=True)
    gathered = lax.all_gather(gathered, "y", axis=0, tiled=True)
    gathered = lax.all_gather(gathered, "z", axis=0, tiled=True)
    own_block = gathered[:, :width]
    edge_block = gathered[:, width:]

    def apply_link(vector):
        ahead_part = from_next(vector)
        outgoing = times(vector, edge_block, 0)
        lower_part = from_previous(outgoing)
        result = times(vector, own_block, 1)
        result = result + 0.5 * times(ahead_part, edge_block, 1)
        return result + 0.5 * lower_part

    def dots(*pairs):
        local = jnp.stack([jnp.sum(a * b, axis=1) for a, b in pairs])
        return lax.psum(local, BLOCK_AXES)

    mask_row = typed_mask.astype(F32)[None, :]
    right_side = mask_row * z_scores

    residual = right_side
    linked = apply_link(mask_row * residual)
    image = mask_row * linked + RIDGE * residual
    norm_now, curvature = dots((residual, residual), (residual, image))
    direction = residual
    step_size = (norm_now / curvature)[:, None]
    solution = step_size * direction
    projected = step_size * linked
    for iteration in range(1, ITERS):
        residual = residual - step_size * image
        fresh_link = apply_link(mask_row * residual)
        fresh_image = mask_row * fresh_link + RIDGE * residual
        norm_next, fresh_curve, cross_a, cross_b, old_curve = dots(
            (residual, residual),
            (residual, fresh_image),
            (residual, image),
            (direction, fresh_image),
            (direction, image),
        )
        ratio = norm_next / norm_now
        curvature = fresh_curve + ratio * (cross_a + cross_b) + ratio * ratio * old_curve
        step_size = (norm_next / curvature)[:, None]
        direction = residual + ratio[:, None] * direction
        image = fresh_image + ratio[:, None] * image
        linked = fresh_link + ratio[:, None] * linked
        solution = solution + step_size * direction
        projected = projected + step_size * linked
        norm_now = norm_next
    imputed = jnp.where(typed_mask[None, :] == 1, z_scores, projected)
    return (solution, imputed)


def solution(mesh):
    fine = Mesh(mesh.devices.reshape(8, 4, 2, 2, 2), SAMPLE_AXES + BLOCK_AXES)
    placed = (P(SAMPLE_AXES, BLOCK_AXES), P(BLOCK_AXES), P(SAMPLE_AXES, BLOCK_AXES))
    return jax.shard_map(
        on_device,
        mesh=fine,
        in_specs=placed,
        out_specs=(P(SAMPLE_AXES, BLOCK_AXES), P(SAMPLE_AXES, BLOCK_AXES)),
        check_vma=False,
    )
```

time: 946 us -> 292 us (0.31)
  waiting for transfers between devices: 558 us -> 133 us
  starting transfers between devices: 154 us -> 33.1 us
  blocking collectives: 172 us -> 79.5 us
  matrix products: 38.4 us -> 23.4 us
    reduce_scatter x1 -> x3, waiting for transfers between devices: 280 us -> 55.7 us  [the longest x1 21.1 us: on_device(): within = lax.psum_scatter(centred, 'z', scatter_dimension=0, tiled=True)]
    all_gather x1, waiting for transfers between devices: 252 us -> 48 us  [on_device(): gathered = lax.all_gather(gathered, 'z', axis=0, tiled=True)]
    psum x6 -> x3, blocking collectives: 172 us -> 19.9 us  [dots(): return lax.psum(local, BLOCK_AXES)]
    ppermute x9 -> x7, starting transfers between devices: 154 us -> 32.9 us  [the longest x4 18.3 us: from_next(): lax.ppermute(block, BLOCK_AXES, [(i + 1, i) for i in range(N_BLOCKS - 1)])]
    all_gather x0 -> x5, blocking collectives: none -> 59.6 us  [the longest x3 44.3 us: gather_stats(): packed = lax.all_gather(packed, axis, axis=0, tiled=True)]
    dot_general x12 -> x10, matrix products: 31.4 us -> 16.9 us  [the longest x9 15.6 us: times(): lax.dot_general(split3(vector), matrix, (((1,), (side,)), ((), ())), pref...]
    ppermute x9 -> x7, waiting for transfers between devices: 26.2 us -> 28.8 us  [the longest x4 28.8 us: from_next(): lax.ppermute(block, BLOCK_AXES, [(i + 1, i) for i in range(N_BLOCKS - 1)])]
  transfers between devices with their start and end apart: 11 -> 11, of which waited for: 3 -> 6; matrix products, arithmetic and copies ran while one was open for 2% -> 5% of each run, Pallas kernels for 0% -> 0%
where the time goes in v1:
time: 292 us
  waiting for transfers between devices  133 us (46%)
  blocking collectives  79.5 us (27%)
  starting transfers between devices  33.1 us (11%)
  matrix products  23.4 us (8%)
  between operations  14.2 us (5%)
  other arithmetic  8.64 us (3%)
    all_gather x1, waiting for transfers between devices, on_device(): gathered = lax.all_gather(gathered, 'z', axis=0, tiled=True)  48 us
    all_gather x3, blocking collectives, gather_stats(): packed = lax.all_gather(packed, axis, axis=0, tiled=True)  44.3 us
    ppermute x4, waiting for transfers between devices, from_next(): lax.ppermute(block, BLOCK_AXES, [(i + 1, i) for i in range(N_BLOCKS - 1)])  28.8 us
    reduce_scatter x1, waiting for transfers between devices, on_device(): within = lax.psum_scatter(centred, 'z', scatter_dimension=0, tiled=True)  21.1 us
    reduce_scatter x1, waiting for transfers between devices, on_device(): within = lax.psum_scatter(within, 'xl', scatter_dimension=0, tiled=True)  20.2 us
    psum x3, blocking collectives, dots(): return lax.psum(local, BLOCK_AXES)  19.9 us
    ppermute x4, starting transfers between devices, from_next(): lax.ppermute(block, BLOCK_AXES, [(i + 1, i) for i in range(N_BLOCKS - 1)])  18.3 us
    dot_general x9, matrix products, times(): lax.dot_general(split3(vector), matrix, (((1,), (side,)), ((), ())), pref...  15.6 us
  transfers between devices with their start and end apart: 11, of which 6 were waited for; matrix products, arithmetic and copies ran while one was open for 5% of the time, Pallas kernels for 0%

profile of v1, /device:TPU:1, one launch (start us, length us, event | category | flops | bytes accessed | tf_op | source)
XLA Modules:
  0.0 291.5 jit_solution(16057749935253873127)
XLA Ops:
  7.2 2.8 add_convert_fusion
  10.0 5.1 %collective-permute-start = (bf16[1024,1024]{1,0:T(8,128)(2,1)S(1)}, bf16[1024,1024]{1,0:T(8,128)(2,1)S(1)}, u32[]{:S(2)}, u32[]{:S(2)}) collective-permute-start(bf16[1024,1024]{1,0:T(8,128)(2,1)S(1)} %add_convert_fusion), channel_id=1, source_target_pairs={{1,0},{2,1},{3,2},{5,4},{6,5},{7,6},{9,8},{10,9},{11,10},{13,12},{... | collective-permute-start | bytes 6291464 | tf_op jit(solution)/shard_map/ppermute | solution.py:19
  15.1 24.6 %collective-permute-done = bf16[1024,1024]{1,0:T(8,128)(2,1)S(1)} collective-permute-done((bf16[1024,1024]{1,0:T(8,128)(2,1)S(1)}, bf16[1024,1024]{1,0:T(8,128)(2,1)S(1)}, u32[]{:S(2)}, u32[]{:S(2)}) %collective-permute-start) | collective-permute-done | bytes 2097184 | tf_op jit(solution)/shard_map/ppermute | solution.py:19
  41.1 6.5 %subtract_convert_fusion = bf16[1024,2048]{1,0:T(8,128)(2,1)} fusion(f32[2048]{0:T(1024)S(1)} %broadcast_multiply_fusion.3, f32[1024]{0:T(1024)S(1)} %bitcast.95, bf16[1024,1024]{1,0:T(8,128)(2,1)S(1)} %add_convert_fusion, bf16[1024,1024]{1,0:T(8,128)(2,1)S(1)} %collective-permute-done), kind=kOutput, calls=%fused_computation.3 | convolution fusion | flops 4309647360 | bytes 8400896 | tf_op jit(solution)/shard_map/dot_general | solution.py:27
  47.7 23.4 %all-gather.3 = f32[8,2,2048]{2,1,0:T(2,128)S(1)} all-gather(f32[1,2,2048]{2,1,0:T(2,128)S(1)} %maximum_bitcast_fusion.2), channel_id=2, replica_groups=mesh['z'=8,'y'=4,'xl'=2,'xh'=2,'core'=2] {'z'}, dimensions={0}, use_global_device_ids=true | all-gather | bytes 147456 | tf_op jit(solution)/shard_map/all_gather | solution.py:59
  71.3 11.7 %all-gather.4 = f32[4,9,2048]{2,1,0:T(8,128)S(1)} all-gather(f32[1,9,2048]{2,1,0:T(8,128)S(1)} %maximum_bitcast_fusion.1), channel_id=3, replica_groups=mesh['z'=8,'y'=4,'xl'=2,'xh'=2,'core'=2] {'y'}, dimensions={0}, use_global_device_ids=true | all-gather | bytes 368640 | tf_op jit(solution)/shard_map/all_gather | solution.py:59
  83.0 21.1 %reduce-scatter.4.cloned.1.call-done = bf16[128,2048]{1,0:T(8,128)(2,1)} async-done(((bf16[1024,2048]{1,0:T(8,128)(2,1)}), bf16[128,2048]{1,0:T(8,128)(2,1)}) %reduce-scatter.4.cloned.1.call-update) | async-done | bytes 524304 | tf_op jit(solution)/shard_map/reduce_scatter | solution.py:98
  106.4 9.2 %all-gather.5 = f32[2,33,2048]{2,1,0:T(8,128)S(1)} all-gather(f32[1,33,2048]{2,1,0:T(8,128)S(1)} %maximum_bitcast_fusion), channel_id=4, replica_groups=mesh['z'=8,'y'=4,'xl'=2,'xh'=2,'core'=2] {'xl'}, dimensions={0}, use_global_device_ids=true | all-gather | bytes 811008 | tf_op jit(solution)/shard_map/all_gather | solution.py:59
  115.9 14.4 %reduce-scatter.6.cloned.1.call-done = f32[32,2048]{1,0:T(8,128)} async-done(((f32[128,2048]{1,0:T(8,128)}), f32[32,2048]{1,0:T(8,128)}) %reduce-scatter.6.cloned.1.call-update) | async-done | bytes 262160 | tf_op jit(solution)/shard_map/reduce_scatter | solution.py:99
  130.5 20.2 %reduce-scatter.8.cloned.1.call-done = f32[16,2048]{1,0:T(8,128)} async-done(((f32[32,2048]{1,0:T(8,128)}), f32[16,2048]{1,0:T(8,128)}) %reduce-scatter.8.cloned.1.call-update) | async-done | bytes 131088 | tf_op jit(solution)/shard_map/reduce_scatter | solution.py:100
  152.0 3.8 %all_gather.21 = bf16[32,2048]{1,0:T(8,128)(2,1)S(1)} all-gather(bf16[16,2048]{1,0:T(8,128)(2,1)S(1)} %fusion.4), channel_id=1, replica_groups=mesh['z'=8,'y'=4,'xl'=2,'xh'=2,'core'=2] {'xl'}, dimensions={0}, use_global_device_ids=true | all-gather | bytes 196608 | tf_op jit(solution)/shard_map/all_gather | solution.py:117
  155.8 11.5 %all_gather.22 = bf16[128,2048]{1,0:T(8,128)(2,1)} all-gather(bf16[32,2048]{1,0:T(8,128)(2,1)S(1)} %all_gather.21), channel_id=1, replica_groups=mesh['z'=8,'y'=4,'xl'=2,'xh'=2,'core'=2] {'y'}, dimensions={0}, use_global_device_ids=true | all-gather | bytes 655360 | tf_op jit(solution)/shard_map/all_gather | solution.py:118
  167.3 6.7 %collective-permute-start.1 = (f32[16,1024]{1,0:T(8,128)S(1)}, f32[16,1024]{1,0:T(8,128)S(1)}, u32[]{:S(2)}, u32[]{:S(2)}) collective-permute-start(f32[16,1024]{1,0:T(8,128)S(1)} %get-tuple-element.28), channel_id=1, source_target_pairs={{1,0},{2,1},{3,2},{5,4},{6,5},{7,6},{9,8},{10,9},{11,10},{13,12},{... | collective-permute-start | bytes 196616 | tf_op jit(solution)/shard_map/ppermute | solution.py:19
  174.1 4.2 %collective-permute-done.1 = f32[16,1024]{1,0:T(8,128)S(1)} collective-permute-done((f32[16,1024]{1,0:T(8,128)S(1)}, f32[16,1024]{1,0:T(8,128)S(1)}, u32[]{:S(2)}, u32[]{:S(2)}) %collective-permute-start.1) | collective-permute-done | bytes 65568 | tf_op jit(solution)/shard_map/ppermute | solution.py:19
  178.3 48.0 %all-gather.8.cloned.1.call-done = bf16[1024,2048]{1,0:T(8,128)(2,1)} async-done(((bf16[128,2048]{1,0:T(8,128)(2,1)}), bf16[1024,2048]{1,0:T(8,128)(2,1)}) %all-gather.8.cloned.1.call-update) | async-done | bytes 4194320 | tf_op jit(solution)/shard_map/all_gather | solution.py:119
  228.6 5.3 %collective-permute-start.2 = (f32[16,1024]{1,0:T(8,128)S(1)}, f32[16,1024]{1,0:T(8,128)S(1)}, u32[]{:S(2)}, u32[]{:S(2)}) collective-permute-start(f32[16,1024]{1,0:T(8,128)S(1)} %slice_add_fusion.12), channel_id=1, source_target_pairs={{0,1},{1,2},{2,3},{4,5},{5,6},{6,7},{8,9},{9,10},{10,11},{12,13},{... | collective-permute-start | bytes 196616 | tf_op jit(solution)/shard_map/ppermute | solution.py:23
  233.9 2.3 fusion.9
  237.2 6.6 %psum.21 = f32[2,16]{1,0:T(2,128)S(1)} all-reduce(f32[2,16]{1,0:T(2,128)S(1)} %pad_maximum_fusion.11), channel_id=1, replica_groups=mesh['z'=8,'y'=4,'xl'=2,'xh'=2,'core'=2] {'xh','core'}, use_global_device_ids=true, to_apply=%region_11.12 | all-reduce | flops 32 | bytes 256 | tf_op jit(solution)/shard_map/psum | solution.py:133
  244.0 3.2 %collective-permute-start.3 = (f32[16,1024]{1,0:T(8,128)S(1)}, f32[16,1024]{1,0:T(8,128)S(1)}, u32[]{:S(2)}, u32[]{:S(2)}) collective-permute-start(f32[16,1024]{1,0:T(8,128)S(1)} %get-tuple-element.25), channel_id=1, source_target_pairs={{1,0},{2,1},{3,2},{5,4},{6,5},{7,6},{9,8},{10,9},{11,10},{13,12},{... | collective-permute-start | bytes 196616 | tf_op jit(solution)/shard_map/ppermute | solution.py:19
  249.3 4.7 %collective-permute-start.4 = (f32[16,1024]{1,0:T(8,128)S(1)}, f32[16,1024]{1,0:T(8,128)S(1)}, u32[]{:S(2)}, u32[]{:S(2)}) collective-permute-start(f32[16,1024]{1,0:T(8,128)S(1)} %slice_add_fusion.6), channel_id=1, source_target_pairs={{0,1},{1,2},{2,3},{4,5},{5,6},{6,7},{8,9},{9,10},{10,11},{12,13},{... | collective-permute-start | bytes 196616 | tf_op jit(solution)/shard_map/ppermute | solution.py:23
  257.4 6.6 %psum.22 = f32[5,16]{1,0:T(8,128)S(1)} all-reduce(f32[5,16]{1,0:T(8,128)S(1)} %stack.50), channel_id=1, replica_groups=mesh['z'=8,'y'=4,'xl'=2,'xh'=2,'core'=2] {'xh','core'}, use_global_device_ids=true, to_apply=%region_16.17 | all-reduce | flops 80 | bytes 640 | tf_op jit(solution)/shard_map/psum | solution.py:133
  264.1 3.2 %collective-permute-start.5 = (f32[16,1024]{1,0:T(8,128)S(1)}, f32[16,1024]{1,0:T(8,128)S(1)}, u32[]{:S(2)}, u32[]{:S(2)}) collective-permute-start(f32[16,1024]{1,0:T(8,128)S(1)} %get-tuple-element.19), channel_id=1, source_target_pairs={{1,0},{2,1},{3,2},{5,4},{6,5},{7,6},{9,8},{10,9},{11,10},{13,12},{... | collective-permute-start | bytes 196616 | tf_op jit(solution)/shard_map/ppermute | solution.py:19
  269.5 4.7 %collective-permute-start.6 = (f32[16,1024]{1,0:T(8,128)S(1)}, f32[16,1024]{1,0:T(8,128)S(1)}, u32[]{:S(2)}, u32[]{:S(2)}) collective-permute-start(f32[16,1024]{1,0:T(8,128)S(1)} %slice_add_fusion), channel_id=1, source_target_pairs={{0,1},{1,2},{2,3},{4,5},{5,6},{6,7},{8,9},{9,10},{10,11},{12,13},{... | collective-permute-start | bytes 196616 | tf_op jit(solution)/shard_map/ppermute | solution.py:23
  277.6 6.6 %psum.23 = f32[5,16]{1,0:T(8,128)S(1)} all-reduce(f32[5,16]{1,0:T(8,128)S(1)} %stack.56), channel_id=1, replica_groups=mesh['z'=8,'y'=4,'xl'=2,'xh'=2,'core'=2] {'xh','core'}, use_global_device_ids=true, to_apply=%region_22.23 | all-reduce | flops 80 | bytes 640 | tf_op jit(solution)/shard_map/psum | solution.py:133
  (74 shorter events, 20.8 us)
Async XLA Ops:
  7.2 97.0 %reduce-scatter.4.cloned.1.call-start = ((), (), s32[]{:S(2)}) async-start(), calls=%async_computation.3 | async-start | bytes 4718592 | tf_op jit(solution)/shard_map/reduce_scatter | solution.py:98
  10.0 29.7 %collective-permute-start = (bf16[1024,1024]{1,0:T(8,128)(2,1)S(1)}, bf16[1024,1024]{1,0:T(8,128)(2,1)S(1)}, u32[]{:S(2)}, u32[]{:S(2)}) collective-permute-start(bf16[1024,1024]{1,0:T(8,128)(2,1)S(1)} %add_convert_fusion), channel_id=1, source_target_pairs={{1,0},{2,1},{3,2},{5,4},{6,5},{7,6},{9,8},{10,9},{11,10},{13,12},{... | collective-permute-start | bytes 6291464 | tf_op jit(solution)/shard_map/ppermute | solution.py:19
  47.6 82.6 %reduce-scatter.6.cloned.1.call-start = ((), (), s32[]{:S(2)}) async-start(), calls=%async_computation.4 | async-start | bytes 1310720 | tf_op jit(solution)/shard_map/reduce_scatter | solution.py:99
  106.3 61.0 %copy-start.1 = (s32[1024]{0:T(1024)S(1)}, s32[1024]{0:T(1024)}, u32[]{:S(2)}) copy-start(s32[1024]{0:T(1024)} %param.4) | copy-start | bytes 12292
  106.3 61.1 %copy-start = (f32[16,1024]{1,0:T(8,128)S(1)}, f32[16,1024]{1,0:T(8,128)}, u32[]{:S(2)}) copy-start(f32[16,1024]{1,0:T(8,128)} %param.5) | copy-start | bytes 196612
  106.3 44.3 %reduce-scatter.8.cloned.1.call-start = ((), (), s32[]{:S(2)}) async-start(), calls=%async_computation.5 | async-start | bytes 393216 | tf_op jit(solution)/shard_map/reduce_scatter | solution.py:100
  130.3 96.1 %all-gather.8.cloned.1.call-start = ((), (), s32[]{:S(2)}) async-start(), calls=%async_computation.6 | async-start | bytes 4718592 | tf_op jit(solution)/shard_map/all_gather | solution.py:119
  167.3 11.0 %collective-permute-start.1 = (f32[16,1024]{1,0:T(8,128)S(1)}, f32[16,1024]{1,0:T(8,128)S(1)}, u32[]{:S(2)}, u32[]{:S(2)}) collective-permute-start(f32[16,1024]{1,0:T(8,128)S(1)} %get-tuple-element.28), channel_id=1, source_target_pairs={{1,0},{2,1},{3,2},{5,4},{6,5},{7,6},{9,8},{10,9},{11,10},{13,12},{... | collective-permute-start | bytes 196616 | tf_op jit(solution)/shard_map/ppermute | solution.py:19
  226.3 9.9 %copy-start.2 = (bf16[1024,2048]{1,0:T(8,128)(2,1)S(1)}, bf16[1024,2048]{1,0:T(8,128)(2,1)}, u32[]{:S(2)}) copy-start(bf16[1024,2048]{1,0:T(8,128)(2,1)} %all-gather.8.cloned.1.call-done) | copy-start | bytes 12582916
  228.6 8.4 %collective-permute-start.2 = (f32[16,1024]{1,0:T(8,128)S(1)}, f32[16,1024]{1,0:T(8,128)S(1)}, u32[]{:S(2)}, u32[]{:S(2)}) collective-permute-start(f32[16,1024]{1,0:T(8,128)S(1)} %slice_add_fusion.12), channel_id=1, source_target_pairs={{0,1},{1,2},{2,3},{4,5},{5,6},{6,7},{8,9},{9,10},{10,11},{12,13},{... | collective-permute-start | bytes 196616 | tf_op jit(solution)/shard_map/ppermute | solution.py:23
  243.8 12.5 %copy-start.3 = (bf16[1024,2048]{1,0:T(8,128)(2,1)S(1)}, bf16[1024,2048]{1,0:T(8,128)(2,1)}, u32[]{:S(2)}) copy-start(bf16[1024,2048]{1,0:T(8,128)(2,1)} %all-gather.8.cloned.1.call-done) | copy-start | bytes 12582916
  244.0 12.3 %collective-permute-start.3 = (f32[16,1024]{1,0:T(8,128)S(1)}, f32[16,1024]{1,0:T(8,128)S(1)}, u32[]{:S(2)}, u32[]{:S(2)}) collective-permute-start(f32[16,1024]{1,0:T(8,128)S(1)} %get-tuple-element.25), channel_id=1, source_target_pairs={{1,0},{2,1},{3,2},{5,4},{6,5},{7,6},{9,8},{10,9},{11,10},{13,12},{... | collective-permute-start | bytes 196616 | tf_op jit(solution)/shard_map/ppermute | solution.py:19
  249.3 7.8 %collective-permute-start.4 = (f32[16,1024]{1,0:T(8,128)S(1)}, f32[16,1024]{1,0:T(8,128)S(1)}, u32[]{:S(2)}, u32[]{:S(2)}) collective-permute-start(f32[16,1024]{1,0:T(8,128)S(1)} %slice_add_fusion.6), channel_id=1, source_target_pairs={{0,1},{1,2},{2,3},{4,5},{5,6},{6,7},{8,9},{9,10},{10,11},{12,13},{... | collective-permute-start | bytes 196616 | tf_op jit(solution)/shard_map/ppermute | solution.py:23
  264.0 12.5 %copy-start.4 = (bf16[1024,2048]{1,0:T(8,128)(2,1)S(1)}, bf16[1024,2048]{1,0:T(8,128)(2,1)}, u32[]{:S(2)}) copy-start(bf16[1024,2048]{1,0:T(8,128)(2,1)} %all-gather.8.cloned.1.call-done) | copy-start | bytes 12582916
  264.1 12.3 %collective-permute-start.5 = (f32[16,1024]{1,0:T(8,128)S(1)}, f32[16,1024]{1,0:T(8,128)S(1)}, u32[]{:S(2)}, u32[]{:S(2)}) collective-permute-start(f32[16,1024]{1,0:T(8,128)S(1)} %get-tuple-element.19), channel_id=1, source_target_pairs={{1,0},{2,1},{3,2},{5,4},{6,5},{7,6},{9,8},{10,9},{11,10},{13,12},{... | collective-permute-start | bytes 196616 | tf_op jit(solution)/shard_map/ppermute | solution.py:19
  269.5 7.8 %collective-permute-start.6 = (f32[16,1024]{1,0:T(8,128)S(1)}, f32[16,1024]{1,0:T(8,128)S(1)}, u32[]{:S(2)}, u32[]{:S(2)}) collective-permute-start(f32[16,1024]{1,0:T(8,128)S(1)} %slice_add_fusion), channel_id=1, source_target_pairs={{0,1},{1,2},{2,3},{4,5},{5,6},{6,7},{8,9},{9,10},{10,11},{12,13},{... | collective-permute-start | bytes 196616 | tf_op jit(solution)/shard_map/ppermute | solution.py:23
Sparse Core Ops, SparseCore 0:
  47.7 56.3 reduce-scatter.3
  106.7 23.5 reduce-scatter.5
  132.7 17.8 reduce-scatter.7
  167.4 58.8 all-gather.7
